TPU v7x, 128 devices: a whole 4x4x4 slice. The times are simulated.
128 devices in a mesh: node: 32 (over y, x, core), rhs: 4 (over z).
Axes of the slice: x: 4, y: 4, z: 4, core: 2. Of those that a mesh axis runs over, the one named last changes fastest.
Arguments:
- right_side: float32 [64, 5, 256, 128], P('rhs', None, 'node'), may hold values from -6 to 6
- diag_tiles: bfloat16 [5, 256, 128, 128], P(None, ('node', 'rhs')), may hold values from -0.25 to 1.65
- off_tiles: bfloat16 [4, 256, 4, 128, 128], P(None, ('node', 'rhs')), may hold values from -0.125 to 0.125
- src_part: int32 [4, 256, 4], P(None, 'node'), may hold values from 0 to 31, all different within a row; in each aligned block of 8 rows (0 to 7, 8 to 15, ..., all dimensions but the last counted through in order) at most 2 rows name the same one
- src_slot: int32 [4, 256, 4], P(None, 'node'), may hold values from 0 to 7
Outputs:
- solution: float32 [64, 5, 256, 128], P('rhs', None, 'node')
Inputs may be any that keep to these rules, and one draw needn't show every extreme that they name: `src_part`: over the 8 block rows of one partition at one level, each row names 4 different partitions, and no partition is named by more than 2 rows.
All inputs are finite; a program needn't handle non-finite values.
Results may differ from a plain program's by a relative error of at most 0.006.
Values may be sent and summed in bfloat16 or wider, within the bound.
A program may use at most 64 MiB of HBM per device.

v0:
```python
import jax
import jax.numpy as jnp
from jax import lax
from jax.sharding import PartitionSpec as P


def sweeps(vectors, diag_whole, off_whole, owner, slot, peers, fetch_dense, push_dense):
    columns, levels, rows_here, block_size = vectors.shape
    linked = owner.shape[0]
    fanout = owner.shape[2]
    flat_index = (owner * rows_here + slot).reshape(linked, rows_here * fanout)
    stored = []
    previous = None
    for level_at in range(levels):
        current = vectors[:, level_at]
        if level_at > 0:
            gathered = fetch_dense(previous)
            referenced = jnp.take(gathered, flat_index[level_at - 1], axis=1)
            referenced = referenced.reshape(columns, rows_here, fanout, block_size)
            coupled = jnp.einsum(
                "cbks,bkts->cbt",
                referenced,
                off_whole[level_at - 1],
                preferred_element_type=jnp.float32,
            )
            current = current - coupled
        rounded = current.astype(jnp.bfloat16)
        previous = jnp.einsum(
            "cbs,bts->cbt", rounded, diag_whole[level_at], preferred_element_type=jnp.float32
        ).astype(jnp.bfloat16)
        stored.append(previous)
    results = [None] * levels
    upper_round = None
    for level_at in range(levels - 1, -1, -1):
        if level_at < levels - 1:
            contrib_terms = jnp.einsum(
                "cbt,bkts->cbks",
                upper_round,
                off_whole[level_at],
                preferred_element_type=jnp.float32,
            )
            contrib_terms = contrib_terms.reshape(columns, rows_here * fanout, block_size)
            spread = jnp.zeros((columns, peers * rows_here, block_size), jnp.float32)
            spread = spread.at[:, flat_index[level_at]].add(contrib_terms)
            incoming = push_dense(spread)
            back_in = (stored[level_at].astype(jnp.float32) - incoming).astype(jnp.bfloat16)
        else:
            back_in = stored[level_at]
        solution = jnp.einsum(
            "cbs,bst->cbt", back_in, diag_whole[level_at], preferred_element_type=jnp.float32
        )
        upper_round = solution.astype(jnp.bfloat16)
        results[level_at] = solution
    return jnp.stack(results, axis=1)


def on_device(right_side, diag_tiles, off_tiles, src_part, src_slot):
    partitions = lax.axis_size("node")
    diag_whole, off_whole = (
        lax.all_gather(diag_tiles, "rhs", axis=1, tiled=True),
        lax.all_gather(off_tiles, "rhs", axis=1, tiled=True),
    )
    return sweeps(
        right_side,
        diag_whole,
        off_whole,
        src_part,
        src_slot,
        partitions,
        lambda x: lax.all_gather(x, "node", axis=1, tiled=True),
        lambda x: lax.psum_scatter(x, "node", scatter_dimension=1, tiled=True),
    )


def solution(mesh):
    placed = (
        P("rhs", None, "node", None),
        P(None, ("node", "rhs"), None, None),
        P(None, ("node", "rhs"), None, None, None),
        P(None, "node", None),
        P(None, "node", None),
    )
    return jax.shard_map(
        on_device,
        mesh=mesh,
        in_specs=placed,
        out_specs=P("rhs", None, "node", None),
        check_vma=False,
    )
```

profile of v0, /device:TPU:0, one launch (start us, length us, event | category | flops | bytes accessed | tf_op | source)
XLA Modules:
  0.0 627.2 jit_solution(13265562975064454400)
XLA Ops:
  6.5 0.7 all-gather.7.cloned.1.call-update
  7.3 0.8 slice.99
  8.2 28.5 %all-gather.7.cloned.1.call-done = bf16[5,8,128,128]{3,2,1,0:T(8,128)(2,1)} async-done(((bf16[5,2,128,128]{3,2,1,0:T(8,128)(2,1)}), bf16[5,8,128,128]{3,2,1,0:T(8,128)(2,1)}) %all-gather.7.cloned.1.call-update) | async-done | bytes 1310736 | tf_op jit(solution)/shard_map/all_gather | solution.py:60
  36.6 1.9 fusion.9
  38.6 0.7 all-gather.11.cloned.1.call-update
  39.4 0.7 multiply_add_fusion
  40.1 0.1 copy.33
  40.2 0.1 squeeze.76
  40.3 41.7 %all-gather.9.cloned.1.call-done = bf16[16,256,128]{2,0,1:T(8,128)(2,1)} async-done(((bf16[16,8,128]{2,0,1:T(8,128)(2,1)}), bf16[16,256,128]{2,0,1:T(8,128)(2,1)}) %all-gather.9.cloned.1.call-update) | async-done | bytes 1048592 | tf_op jit(solution)/shard_map/all_gather | solution.py:70
  82.0 1.8 gather_fusion
  83.9 0.1 broadcast_select_fusion.3
  84.0 47.6 %all-gather.11.cloned.1.call-done = bf16[4,8,4,128,128]{4,3,2,1,0:T(8,128)(2,1)} async-done(((bf16[4,2,4,128,128]{4,3,2,1,0:T(8,128)(2,1)}), bf16[4,8,4,128,128]{4,3,2,1,0:T(8,128)(2,1)}) %all-gather.11.cloned.1.call-update) | async-done | bytes 4194320 | tf_op jit(solution)/shard_map/all_gather | solution.py:61
  131.6 2.4 fusion.10
  134.0 0.1 copy.36
  134.1 0.1 squeeze.81
  134.2 42.7 %all-gather.13.cloned.1.call-done = bf16[16,256,128]{2,0,1:T(8,128)(2,1)} async-done(((bf16[16,8,128]{2,0,1:T(8,128)(2,1)}), bf16[16,256,128]{2,0,1:T(8,128)(2,1)}) %all-gather.13.cloned.1.call-update) | async-done | bytes 1048592 | tf_op jit(solution)/shard_map/all_gather | solution.py:70
  177.0 1.8 gather_fusion.1
  178.8 0.1 broadcast_select_fusion.2
  178.9 2.4 fusion.11
  181.3 0.1 copy.39
  181.4 0.1 squeeze.86
  181.5 41.9 %all-gather.15.cloned.1.call-done = bf16[16,256,128]{2,0,1:T(8,128)(2,1)} async-done(((bf16[16,8,128]{2,0,1:T(8,128)(2,1)}), bf16[16,256,128]{2,0,1:T(8,128)(2,1)}) %all-gather.15.cloned.1.call-update) | async-done | bytes 1048592 | tf_op jit(solution)/shard_map/all_gather | solution.py:70
  223.4 1.8 gather_fusion.2
  225.3 0.1 broadcast_select_fusion.1
  225.4 2.4 fusion.12
  227.8 0.1 copy.42
  227.9 0.1 squeeze.91
  228.0 0.1 squeeze.89
  228.1 41.8 %all-gather.17.cloned.1.call-done = bf16[16,256,128]{2,0,1:T(8,128)(2,1)} async-done(((bf16[16,8,128]{2,0,1:T(8,128)(2,1)}), bf16[16,256,128]{2,0,1:T(8,128)(2,1)}) %all-gather.17.cloned.1.call-update) | async-done | bytes 1048592 | tf_op jit(solution)/shard_map/all_gather | solution.py:70
  269.9 1.8 gather_fusion.3
  271.7 0.1 broadcast_select_fusion
  271.8 1.6 fusion.8
  273.4 0.4 fusion.14
  273.8 2.2 fusion.18
  276.0 0.1 broadcast.68.clone.2
  276.1 3.0 scatter_fusion
  279.2 1.3 copy-done.1
  280.6 0.0 reduce-scatter.7.cloned.1.call-start
  280.6 0.1 squeeze.84
  280.7 78.1 %reduce-scatter.5.cloned.1.call-done = f32[16,8,128]{2,0,1:T(8,128)} async-done(((f32[16,256,128]{2,0,1:T(8,128)}), f32[16,8,128]{2,0,1:T(8,128)}) %reduce-scatter.5.cloned.1.call-update) | async-done | bytes 65552 | tf_op jit(solution)/shard_map/reduce_scatter | solution.py:71
  358.8 1.0 fusion.21
  359.8 2.2 fusion.17
  362.0 0.1 broadcast.68.clone.1
  362.1 3.0 scatter_fusion.1
  365.2 1.3 copy-done.2
  366.6 0.1 squeeze.79
  366.7 78.1 %reduce-scatter.7.cloned.1.call-done = f32[16,8,128]{2,0,1:T(8,128)} async-done(((f32[16,256,128]{2,0,1:T(8,128)}), f32[16,8,128]{2,0,1:T(8,128)}) %reduce-scatter.7.cloned.1.call-update) | async-done | bytes 65552 | tf_op jit(solution)/shard_map/reduce_scatter | solution.py:71
  444.8 1.0 fusion.20
  445.8 2.2 fusion.16
  448.0 0.1 broadcast.68.clone
  448.1 3.0 scatter_fusion.2
  451.2 1.3 copy-done.3
  452.6 0.1 squeeze.74
  452.7 78.1 %reduce-scatter.9.cloned.1.call-done = f32[16,8,128]{2,0,1:T(8,128)} async-done(((f32[16,256,128]{2,0,1:T(8,128)}), f32[16,8,128]{2,0,1:T(8,128)}) %reduce-scatter.9.cloned.1.call-update) | async-done | bytes 65552 | tf_op jit(solution)/shard_map/reduce_scatter | solution.py:71
  530.8 1.0 fusion.19
  531.8 2.2 fusion.15
  534.0 0.1 broadcast.68
  534.2 3.0 scatter_fusion.3
  537.2 1.3 copy-done
  538.6 78.2 %reduce-scatter.11.cloned.1.call-done = f32[16,8,128]{2,0,1:T(8,128)} async-done(((f32[16,256,128]{2,0,1:T(8,128)}), f32[16,8,128]{2,0,1:T(8,128)}) %reduce-scatter.11.cloned.1.call-update) | async-done | bytes 65552 | tf_op jit(solution)/shard_map/reduce_scatter | solution.py:71
  616.8 1.0 fusion
  617.8 0.9 bitcast_dynamic-update-slice_fusion.3
  618.7 0.8 bitcast_dynamic-update-slice_fusion.2
  619.5 0.8 copy.45
  (49 shorter events, 0.6 us)
Async XLA Ops:
  6.5 33.8 %copy-start.7 = (f32[16,5,8,128]{3,2,1,0:T(8,128)S(1)}, f32[16,5,8,128]{3,2,1,0:T(8,128)}, u32[]{:S(2)}) copy-start(f32[16,5,8,128]{3,2,1,0:T(8,128)} %param.7) | copy-start | bytes 983044
  6.5 30.1 %all-gather.7.cloned.1.call-start = ((), (), s32[]{:S(2)}) async-start(), calls=%async_computation.4 | async-start | bytes 1638400 | tf_op jit(solution)/shard_map/all_gather | solution.py:60
  7.3 74.8 %all-gather.9.cloned.1.call-start = ((), (), s32[]{:S(2)}) async-start(), calls=%async_computation.5 | async-start | bytes 1081344 | tf_op jit(solution)/shard_map/all_gather | solution.py:70
  36.6 95.0 %copy-start.4 = (bf16[5,8,128,128]{3,2,1,0:T(8,128)(2,1)S(1)}, bf16[5,8,128,128]{3,2,1,0:T(8,128)(2,1)}, u32[]{:S(2)}) copy-start(bf16[5,8,128,128]{3,2,1,0:T(8,128)(2,1)} %all-gather.7.cloned.1.call-done) | copy-start | bytes 3932164
  38.6 93.0 %all-gather.11.cloned.1.call-start = ((), (), s32[]{:S(2)}) async-start(), calls=%async_computation.6 | async-start | bytes 5242880 | tf_op jit(solution)/shard_map/all_gather | solution.py:61
  39.3 137.6 %all-gather.13.cloned.1.call-start = ((), (), s32[]{:S(2)}) async-start(), calls=%async_computation.7 | async-start | bytes 1081344 | tf_op jit(solution)/shard_map/all_gather | solution.py:70
  134.0 89.4 %all-gather.15.cloned.1.call-start = ((), (), s32[]{:S(2)}) async-start(), calls=%async_computation.8 | async-start | bytes 1081344 | tf_op jit(solution)/shard_map/all_gather | solution.py:70
  181.3 88.6 %all-gather.17.cloned.1.call-start = ((), (), s32[]{:S(2)}) async-start(), calls=%async_computation.9 | async-start | bytes 1081344 | tf_op jit(solution)/shard_map/all_gather | solution.py:70
  227.8 131.0 %reduce-scatter.5.cloned.1.call-start = ((), (), s32[]{:S(2)}) async-start(), calls=%async_computation.10 | async-start | bytes 2162688 | tf_op jit(solution)/shard_map/reduce_scatter | solution.py:71
  279.2 1.4 copy-start.1
  280.6 164.2 %reduce-scatter.7.cloned.1.call-start = ((), (), s32[]{:S(2)}) async-start(), calls=%async_computation.11 | async-start | bytes 2162688 | tf_op jit(solution)/shard_map/reduce_scatter | solution.py:71
  365.2 1.4 copy-start.2
  366.5 164.3 %reduce-scatter.9.cloned.1.call-start = ((), (), s32[]{:S(2)}) async-start(), calls=%async_computation.12 | async-start | bytes 2162688 | tf_op jit(solution)/shard_map/reduce_scatter | solution.py:71
  445.8 2.2 copy-start.5
  451.2 1.4 copy-start.3
  452.6 164.2 %reduce-scatter.11.cloned.1.call-start = ((), (), s32[]{:S(2)}) async-start(), calls=%async_computation.13 | async-start | bytes 2162688 | tf_op jit(solution)/shard_map/reduce_scatter | solution.py:71
  531.8 2.2 copy-start.6
  537.2 1.3 copy-start
Sparse Core Ops, SparseCore 0:
  9.0 27.5 all-gather.6
  38.9 43.0 all-gather.8
  83.7 47.8 all-gather.10
  134.1 42.8 all-gather.12
  181.4 41.9 all-gather.14
  227.9 41.9 all-gather.16
  280.7 78.0 reduce-scatter.4
  366.7 78.0 reduce-scatter.6
  452.7 78.0 reduce-scatter.8
  538.7 78.0 reduce-scatter.10
where the time goes:
time: 628 us; the launch traced here: 627 us
  waiting for transfers between devices  558 us (89%)
  matrix products  23.8 us (4%)
  local copies, waits for them, and re-layouts  17.6 us (3%)
  between operations  13.7 us (2%)
  other arithmetic  13.4 us (2%)
    reduce_scatter x4, waiting for transfers between devices, on_device(): lax.psum_scatter(x, 'node', scatter_dimension=1, tiled=True)  312 us
    all_gather x4, waiting for transfers between devices, on_device(): lax.all_gather(x, 'node', axis=1, tiled=True)  168 us
    all_gather x1, waiting for transfers between devices, on_device(): lax.all_gather(off_tiles, 'rhs', axis=1, tiled=True)  47.6 us
    all_gather x1, waiting for transfers between devices, on_device(): lax.all_gather(diag_tiles, 'rhs', axis=1, tiled=True)  28.5 us
  transfers between devices with their start and end apart: 10, of which 10 were waited for; matrix products, arithmetic and copies ran while one was open for 1% of the time, Pallas kernels for 0%

commit v1 on v0

--- a/solution.py
+++ b/solution.py
@@ -67,7 +67,9 @@
         src_part,
         src_slot,
         partitions,
-        lambda x: lax.all_gather(x, "node", axis=1, tiled=True),
+        lambda x: jnp.concatenate(
+            lax.all_to_all(jnp.stack([x] * lax.axis_size("node")), "node", 0, 0), axis=1
+        ),
         lambda x: lax.psum_scatter(x, "node", scatter_dimension=1, tiled=True),
     )
 

time: 628 us -> 522 us (0.83)
  waiting for transfers between devices: 558 us -> 429 us
  starting transfers between devices: 0.37 us -> 22.2 us
    all_gather x4 -> x0, waiting for transfers between devices: 168 us -> none  [on_device(): lax.all_gather(x, 'node', axis=1, tiled=True)]
    all_to_all x0 -> x4, waiting for transfers between devices: none -> 68.3 us  [on_device(): lax.all_to_all(jnp.stack([x] * lax.axis_size('node')), 'node', 0, 0)]
    all_gather x1, waiting for transfers between devices: 47.6 us -> 22.1 us  [on_device(): lax.all_gather(off_tiles, 'rhs', axis=1, tiled=True)]
    all_to_all x0 -> x4, starting transfers between devices: none -> 22 us  [on_device(): lax.all_to_all(jnp.stack([x] * lax.axis_size('node')), 'node', 0, 0)]
where the time goes in v1:
time: 522 us; the launch traced here: 521 us
  waiting for transfers between devices  429 us (82%)
  starting transfers between devices  22.2 us (4%)
  local copies, waits for them, and re-layouts  21.6 us (4%)
  matrix products  21.2 us (4%)
  between operations  13.8 us (3%)
  other arithmetic  13.4 us (3%)
    reduce_scatter x4, waiting for transfers between devices, on_device(): lax.psum_scatter(x, 'node', scatter_dimension=1, tiled=True)  310 us
    all_to_all x4, waiting for transfers between devices, on_device(): lax.all_to_all(jnp.stack([x] * lax.axis_size('node')), 'node', 0, 0)  68.3 us
    all_gather x1, waiting for transfers between devices, on_device(): lax.all_gather(diag_tiles, 'rhs', axis=1, tiled=True)  27 us
    all_gather x1, waiting for transfers between devices, on_device(): lax.all_gather(off_tiles, 'rhs', axis=1, tiled=True)  22.1 us
    all_to_all x4, starting transfers between devices, on_device(): lax.all_to_all(jnp.stack([x] * lax.axis_size('node')), 'node', 0, 0)  22 us
    scatter-add x4, other arithmetic, sweeps(): spread = spread.at[:, flat_index[level_at]].add(contrib_terms)  12.1 us
  transfers between devices with their start and end apart: 10, of which 10 were waited for; matrix products, arithmetic and copies ran while one was open for 1% of the time, Pallas kernels for 0%

profile of v1, /device:TPU:0, one launch (start us, length us, event | category | flops | bytes accessed | tf_op | source)
XLA Modules:
  0.0 520.8 jit_solution(10018230017432353645)
XLA Ops:
  6.5 0.7 all-gather.3.cloned.1.call-update
  7.3 0.7 all-gather.5.cloned.1.call-update
  8.0 0.9 slice.99
  8.9 0.7 multiply_add_fusion
  9.6 27.0 %all-gather.3.cloned.1.call-done = bf16[5,8,128,128]{3,2,1,0:T(8,128)(2,1)} async-done(((bf16[5,2,128,128]{3,2,1,0:T(8,128)(2,1)}), bf16[5,8,128,128]{3,2,1,0:T(8,128)(2,1)}) %all-gather.3.cloned.1.call-update) | async-done | bytes 1310736 | tf_op jit(solution)/shard_map/all_gather | solution.py:60
  36.6 1.2 fusion.9
  37.9 1.2 stack.20
  39.1 7.1 %all-to-all-start = ((bf16[32,16,8,128]{3,2,1,0:T(8,128)(2,1)}), bf16[32,16,8,128]{3,2,1,0:T(8,128)(2,1)S(1)}, u32[]{:S(2)}, u32[]{:S(2)}) async-start(bf16[32,16,8,128]{3,2,1,0:T(8,128)(2,1)} %stack.20), calls=%async_computation | async-start | bytes 2097152 | tf_op jit(solution)/shard_map/all_to_all | solution.py:71
  46.4 17.1 %all-to-all-done = bf16[32,16,8,128]{3,2,1,0:T(8,128)(2,1)S(1)} async-done(((bf16[32,16,8,128]{3,2,1,0:T(8,128)(2,1)}), bf16[32,16,8,128]{3,2,1,0:T(8,128)(2,1)S(1)}, u32[]{:S(2)}, u32[]{:S(2)}) %all-to-all-start) | async-done | bytes 1048608 | tf_op jit(solution)/shard_map/all_to_all | solution.py:71
  63.5 0.3 copy.109
  63.8 0.7 copy.50
  64.5 0.6 gather_fusion
  65.2 22.1 %all-gather.5.cloned.1.call-done = bf16[4,8,4,128,128]{4,3,2,1,0:T(8,128)(2,1)} async-done(((bf16[4,2,4,128,128]{4,3,2,1,0:T(8,128)(2,1)}), bf16[4,8,4,128,128]{4,3,2,1,0:T(8,128)(2,1)}) %all-gather.5.cloned.1.call-update) | async-done | bytes 4194320 | tf_op jit(solution)/shard_map/all_gather | solution.py:61
  87.3 1.7 fusion.10
  89.0 1.2 stack.21
  90.2 7.1 %all-to-all-start.1 = ((bf16[32,16,8,128]{3,2,1,0:T(8,128)(2,1)}), bf16[32,16,8,128]{3,2,1,0:T(8,128)(2,1)S(1)}, u32[]{:S(2)}, u32[]{:S(2)}) async-start(bf16[32,16,8,128]{3,2,1,0:T(8,128)(2,1)} %stack.21), calls=%async_computation.1 | async-start | bytes 2097152 | tf_op jit(solution)/shard_map/all_to_all | solution.py:71
  97.5 17.1 %all-to-all-done.1 = bf16[32,16,8,128]{3,2,1,0:T(8,128)(2,1)S(1)} async-done(((bf16[32,16,8,128]{3,2,1,0:T(8,128)(2,1)}), bf16[32,16,8,128]{3,2,1,0:T(8,128)(2,1)S(1)}, u32[]{:S(2)}, u32[]{:S(2)}) %all-to-all-start.1) | async-done | bytes 1048608 | tf_op jit(solution)/shard_map/all_to_all | solution.py:71
  114.7 0.3 copy.108
  114.9 0.7 copy.56
  115.6 0.6 gather_fusion.1
  116.3 1.7 fusion.11
  118.1 1.2 stack.22
  119.3 3.9 all-to-all-start.2
  123.5 17.1 %all-to-all-done.2 = bf16[32,16,8,128]{3,2,1,0:T(8,128)(2,1)S(1)} async-done(((bf16[32,16,8,128]{3,2,1,0:T(8,128)(2,1)}), bf16[32,16,8,128]{3,2,1,0:T(8,128)(2,1)S(1)}, u32[]{:S(2)}, u32[]{:S(2)}) %all-to-all-start.2) | async-done | bytes 1048608 | tf_op jit(solution)/shard_map/all_to_all | solution.py:71
  140.6 0.3 copy.107
  140.9 0.7 copy.62
  141.6 0.6 gather_fusion.2
  142.3 1.7 fusion.12
  144.0 1.2 stack.23
  145.3 3.9 all-to-all-start.3
  149.5 17.0 %all-to-all-done.3 = bf16[32,16,8,128]{3,2,1,0:T(8,128)(2,1)S(1)} async-done(((bf16[32,16,8,128]{3,2,1,0:T(8,128)(2,1)}), bf16[32,16,8,128]{3,2,1,0:T(8,128)(2,1)S(1)}, u32[]{:S(2)}, u32[]{:S(2)}) %all-to-all-start.3) | async-done | bytes 1048608 | tf_op jit(solution)/shard_map/all_to_all | solution.py:71
  166.5 0.3 copy.106
  166.8 0.7 copy.68
  167.5 0.6 gather_fusion.3
  168.1 0.1 broadcast_select_fusion
  168.2 1.6 fusion.8
  169.8 0.4 fusion.14
  170.2 2.2 fusion.18
  172.4 0.1 broadcast.76.clone.2
  172.5 3.0 scatter_fusion
  175.5 1.3 copy-done.1
  177.0 75.4 %reduce-scatter.5.cloned.1.call-done = f32[16,8,128]{2,0,1:T(8,128)} async-done(((f32[16,256,128]{2,0,1:T(8,128)}), f32[16,8,128]{2,0,1:T(8,128)}) %reduce-scatter.5.cloned.1.call-update) | async-done | bytes 65552 | tf_op jit(solution)/shard_map/reduce_scatter | solution.py:73
  252.4 1.0 fusion.21
  253.4 2.2 fusion.17
  255.6 0.1 broadcast.76.clone.1
  255.7 3.0 scatter_fusion.1
  258.8 1.3 copy-done.2
  260.3 78.1 %reduce-scatter.7.cloned.1.call-done = f32[16,8,128]{2,0,1:T(8,128)} async-done(((f32[16,256,128]{2,0,1:T(8,128)}), f32[16,8,128]{2,0,1:T(8,128)}) %reduce-scatter.7.cloned.1.call-update) | async-done | bytes 65552 | tf_op jit(solution)/shard_map/reduce_scatter | solution.py:73
  338.4 1.0 fusion.20
  339.4 2.2 fusion.16
  341.6 0.1 broadcast.76.clone
  341.7 3.0 scatter_fusion.2
  344.8 1.3 copy-done.3
  346.3 78.0 %reduce-scatter.9.cloned.1.call-done = f32[16,8,128]{2,0,1:T(8,128)} async-done(((f32[16,256,128]{2,0,1:T(8,128)}), f32[16,8,128]{2,0,1:T(8,128)}) %reduce-scatter.9.cloned.1.call-update) | async-done | bytes 65552 | tf_op jit(solution)/shard_map/reduce_scatter | solution.py:73
  424.4 1.0 fusion.19
  425.4 2.2 fusion.15
  427.6 0.1 broadcast.76
  427.7 3.0 scatter_fusion.3
  430.8 1.3 copy-done
  432.1 78.3 %reduce-scatter.11.cloned.1.call-done = f32[16,8,128]{2,0,1:T(8,128)} async-done(((f32[16,256,128]{2,0,1:T(8,128)}), f32[16,8,128]{2,0,1:T(8,128)}) %reduce-scatter.11.cloned.1.call-update) | async-done | bytes 65552 | tf_op jit(solution)/shard_map/reduce_scatter | solution.py:73
  510.4 1.0 fusion
  511.4 0.9 bitcast_dynamic-update-slice_fusion.3
  512.3 0.8 bitcast_dynamic-update-slice_fusion.2
  513.1 0.8 copy.69
  (69 shorter events, 1.9 us)
Async XLA Ops:
  6.5 30.1 %all-gather.3.cloned.1.call-start = ((), (), s32[]{:S(2)}) async-start(), calls=%async_computation.8 | async-start | bytes 1638400 | tf_op jit(solution)/shard_map/all_gather | solution.py:60
  7.3 80.0 %all-gather.5.cloned.1.call-start = ((), (), s32[]{:S(2)}) async-start(), calls=%async_computation.9 | async-start | bytes 5242880 | tf_op jit(solution)/shard_map/all_gather | solution.py:61
  8.0 38.4 %copy-start.10 = (f32[16,5,8,128]{3,2,1,0:T(8,128)S(1)}, f32[16,5,8,128]{3,2,1,0:T(8,128)}, u32[]{:S(2)}) copy-start(f32[16,5,8,128]{3,2,1,0:T(8,128)} %param.7) | copy-start | bytes 983044
  37.8 8.6 %copy-start.11 = (bf16[16,8,128]{2,0,1:T(8,128)(2,1)}, bf16[16,8,128]{2,0,1:T(8,128)(2,1)S(1)}, u32[]{:S(2)}) copy-start(bf16[16,8,128]{2,0,1:T(8,128)(2,1)S(1)} %fusion.9) | copy-start | bytes 98308
  39.1 24.4 %all-to-all-start = ((bf16[32,16,8,128]{3,2,1,0:T(8,128)(2,1)}), bf16[32,16,8,128]{3,2,1,0:T(8,128)(2,1)S(1)}, u32[]{:S(2)}, u32[]{:S(2)}) async-start(bf16[32,16,8,128]{3,2,1,0:T(8,128)(2,1)} %stack.20), calls=%async_computation | async-start | bytes 2097152 | tf_op jit(solution)/shard_map/all_to_all | solution.py:71
  46.4 40.8 %copy-start.4 = (bf16[5,8,128,128]{3,2,1,0:T(8,128)(2,1)S(1)}, bf16[5,8,128,128]{3,2,1,0:T(8,128)(2,1)}, u32[]{:S(2)}) copy-start(bf16[5,8,128,128]{3,2,1,0:T(8,128)(2,1)} %all-gather.3.cloned.1.call-done) | copy-start | bytes 3932164
  89.0 1.3 copy-start.7
  90.2 24.4 %all-to-all-start.1 = ((bf16[32,16,8,128]{3,2,1,0:T(8,128)(2,1)}), bf16[32,16,8,128]{3,2,1,0:T(8,128)(2,1)S(1)}, u32[]{:S(2)}, u32[]{:S(2)}) async-start(bf16[32,16,8,128]{3,2,1,0:T(8,128)(2,1)} %stack.21), calls=%async_computation.1 | async-start | bytes 2097152 | tf_op jit(solution)/shard_map/all_to_all | solution.py:71
  118.1 1.3 copy-start.8
  119.3 21.3 %all-to-all-start.2 = ((bf16[32,16,8,128]{3,2,1,0:T(8,128)(2,1)}), bf16[32,16,8,128]{3,2,1,0:T(8,128)(2,1)S(1)}, u32[]{:S(2)}, u32[]{:S(2)}) async-start(bf16[32,16,8,128]{3,2,1,0:T(8,128)(2,1)} %stack.22), calls=%async_computation.2 | async-start | bytes 2097152 | tf_op jit(solution)/shard_map/all_to_all | solution.py:71
  144.0 1.3 copy-start.9
  145.3 21.3 %all-to-all-start.3 = ((bf16[32,16,8,128]{3,2,1,0:T(8,128)(2,1)}), bf16[32,16,8,128]{3,2,1,0:T(8,128)(2,1)S(1)}, u32[]{:S(2)}, u32[]{:S(2)}) async-start(bf16[32,16,8,128]{3,2,1,0:T(8,128)(2,1)} %stack.23), calls=%async_computation.3 | async-start | bytes 2097152 | tf_op jit(solution)/shard_map/all_to_all | solution.py:71
  149.2 103.2 %reduce-scatter.5.cloned.1.call-start = ((), (), s32[]{:S(2)}) async-start(), calls=%async_computation.10 | async-start | bytes 2162688 | tf_op jit(solution)/shard_map/reduce_scatter | solution.py:73
  175.5 1.4 copy-start.1
  176.9 161.5 %reduce-scatter.7.cloned.1.call-start = ((), (), s32[]{:S(2)}) async-start(), calls=%async_computation.11 | async-start | bytes 2162688 | tf_op jit(solution)/shard_map/reduce_scatter | solution.py:73
  258.8 1.4 copy-start.2
  260.2 164.2 %reduce-scatter.9.cloned.1.call-start = ((), (), s32[]{:S(2)}) async-start(), calls=%async_computation.12 | async-start | bytes 2162688 | tf_op jit(solution)/shard_map/reduce_scatter | solution.py:73
  339.4 2.2 copy-start.5
  344.8 1.4 copy-start.3
  346.2 164.2 %reduce-scatter.11.cloned.1.call-start = ((), (), s32[]{:S(2)}) async-start(), calls=%async_computation.13 | async-start | bytes 2162688 | tf_op jit(solution)/shard_map/reduce_scatter | solution.py:73
  425.4 2.2 copy-start.6
  430.8 1.3 copy-start
Sparse Core Ops, SparseCore 0:
  9.0 27.5 all-gather.2
  38.3 48.8 all-gather.4
  177.0 75.3 reduce-scatter.4
  260.3 78.0 reduce-scatter.6
  346.3 78.0 reduce-scatter.8
  432.2 78.1 reduce-scatter.10
